TPU v7x, 32 devices: a whole 2x2x4 slice. The times are simulated.
32 devices in a mesh: wide: 8 (over y, x, core), narrow: 4 (over z).
Axes of the slice: x: 2, y: 2, z: 4, core: 2. Of those that a mesh axis runs over, the one named last changes fastest.
Arguments:
- tokens: bfloat16 [128, 512, 768], P(('wide', 'narrow')), may hold values from -6 to 6
- lengths: int32 [128], P(('wide', 'narrow')), may hold values from 128 to 512, as said below
- query_lengths: int32 [128], P(('wide', 'narrow')), may hold values from 2 to 64
- language_ids: int32 [128], P(('wide', 'narrow')), may hold values from 0 to 99
- position_table: bfloat16 [512, 768], P('wide', 'narrow'), may hold values from -3 to 3
- segment_table: bfloat16 [2, 768], replicated, may hold values from -3 to 3
- language_table: bfloat16 [100, 768], replicated, may hold values from -3 to 3
- query_weight: bfloat16 [768, 768], P('wide', 'narrow'), may hold values from -0.21875 to 0.21875
- key_weight: bfloat16 [768, 768], P('wide', 'narrow'), may hold values from -0.21875 to 0.21875
- value_weight: bfloat16 [768, 768], P('wide', 'narrow'), may hold values from -0.21875 to 0.21875
- output_weight: bfloat16 [768, 768], P('wide', 'narrow'), may hold values from -0.875 to 0.875
- query_bias: bfloat16 [768], replicated, may hold values from -2 to 2
- value_bias: bfloat16 [768], replicated, may hold values from -2 to 2
- output_bias: bfloat16 [768], replicated, may hold values from -2 to 2
- first_gain: bfloat16 [768], replicated, may hold values from 0.5 to 1.5
- first_shift: bfloat16 [768], replicated, may hold values from -2 to 2
- up_weight: bfloat16 [768, 3072], P('wide', 'narrow'), may hold values from -0.21875 to 0.21875
- up_bias: bfloat16 [3072], replicated, may hold values from -2 to 2
- down_weight: bfloat16 [3072, 768], P('wide', 'narrow'), may hold values from -0.109375 to 0.109375
- down_bias: bfloat16 [768], replicated, may hold values from -2 to 2
- second_gain: bfloat16 [768], replicated, may hold values from 0.5 to 1.5
- second_shift: bfloat16 [768], replicated, may hold values from -2 to 2
- cotangent: bfloat16 [128, 512, 768], P(('wide', 'narrow')), may hold values from -6 to 6
Outputs:
- layer_out: bfloat16 [128, 512, 768], P(('wide', 'narrow'))
- token_grad: bfloat16 [128, 512, 768], P(('wide', 'narrow'))
- position_grad: float32 [512, 768], P('wide', 'narrow')
- segment_grad: float32 [2, 768], replicated
- language_grad: float32 [100, 768], replicated
- query_weight_grad: float32 [768, 768], P('wide', 'narrow')
- key_weight_grad: float32 [768, 768], P('wide', 'narrow')
- value_weight_grad: float32 [768, 768], P('wide', 'narrow')
- output_weight_grad: float32 [768, 768], P('wide', 'narrow')
- query_bias_grad: float32 [768], replicated
- value_bias_grad: float32 [768], replicated
- output_bias_grad: float32 [768], replicated
- first_gain_grad: float32 [768], replicated
- first_shift_grad: float32 [768], replicated
- up_weight_grad: float32 [768, 3072], P('wide', 'narrow')
- up_bias_grad: float32 [3072], replicated
- down_weight_grad: float32 [3072, 768], P('wide', 'narrow')
- down_bias_grad: float32 [768], replicated
- second_gain_grad: float32 [768], replicated
- second_shift_grad: float32 [768], replicated
Inputs may be any that keep to these rules, and one draw needn't show every extreme that they name: Each pair has lengths live tokens, the rest are padding; some pair fills all 512 positions. `query_lengths`: A pair's queries lie within its live tokens.
All inputs are finite; a program needn't handle non-finite values.
Results may differ from a plain program's by a relative error of at most 0.015.
The roundings to bfloat16 on the way count: a program that leaves them out, or rounds other values in their place, can miss the bound.
Values may be sent and summed in bfloat16 or wider, within the bound.
No kernel may reach another device: no remote copies, remote signals or barrier semaphores. Data moves between devices by JAX's collectives and lax.ppermute only.
A program may use at most 256 MiB of HBM per device.

v0:
```python
import math
import jax
import jax.numpy as jnp
from jax import lax
from jax.sharding import PartitionSpec as P

H = 12
HD = 64
EPSILON = 1e-05


def normalize(inputs, scales, offset):
    average = jnp.mean(inputs, axis=-1, keepdims=True)
    centered = inputs - average
    spread = jnp.mean(centered * centered, axis=-1, keepdims=True)
    return centered * lax.rsqrt(spread + EPSILON) * scales + offset


def matmul(left_side, right_side):
    return jnp.dot(left_side, right_side, preferred_element_type=jnp.float32)


def matmul_first_t(left_side, right_side):
    return lax.dot_general(
        left_side, right_side, (((0,), (0,)), ((), ())), preferred_element_type=jnp.float32
    )


def matmul_second_t(left_side, right_side):
    return lax.dot_general(
        left_side, right_side, (((1,), (1,)), ((), ())), preferred_element_type=jnp.float32
    )


def exact_gelu(inputs):
    return jax.nn.gelu(inputs, approximate=False)


def split_heads(flattened, seq_count, seq_len):
    return (
        flattened.reshape(seq_count, seq_len, H, HD)
        .transpose(0, 2, 1, 3)
        .reshape(seq_count * H, seq_len, HD)
    )


def join_heads(blocks, seq_count, seq_len):
    return (
        blocks.reshape(seq_count, H, seq_len, HD)
        .transpose(0, 2, 1, 3)
        .reshape(seq_count * seq_len, H * HD)
    )


def assemble(stacked, wide_count, narrow_count):
    block_rows = stacked.shape[1]
    block_cols = stacked.shape[2]
    return (
        stacked.reshape(wide_count, narrow_count, block_rows, block_cols)
        .transpose(0, 2, 1, 3)
        .reshape(wide_count * block_rows, narrow_count * block_cols)
    )


def disassemble(whole, wide_count, narrow_count):
    block_rows = whole.shape[0] // wide_count
    block_cols = whole.shape[1] // narrow_count
    return (
        whole.reshape(wide_count, block_rows, narrow_count, block_cols)
        .transpose(0, 2, 1, 3)
        .reshape(wide_count * narrow_count, block_rows, block_cols)
    )


def block_scores(query_rows, key_rows, length):
    factor = 1.0 / math.sqrt(HD)
    products = matmul_second_t(query_rows, key_rows) * factor
    keeping = lax.broadcasted_iota(jnp.int32, products.shape, 1) < length
    return jnp.where(keeping, products, -1e30)


def attend_block(pieces):
    query_rows, key_rows, value_rows, length = pieces
    scores = block_scores(query_rows, key_rows, length)
    row_max = jnp.max(scores, axis=1, keepdims=True)
    weights = jnp.exp(scores - row_max)
    row_total = jnp.sum(weights, axis=1, keepdims=True)
    low_weights = (weights / row_total).astype(jnp.bfloat16)
    context = matmul(low_weights, value_rows)
    return (context, (row_max + jnp.log(row_total))[:, 0])


def attend_back(pieces):
    query_rows, key_rows, value_rows, length, log_totals, grad_context = pieces
    scores = block_scores(query_rows, key_rows, length)
    probabilities = jnp.exp(scores - log_totals[:, None])
    grad_probs = matmul_second_t(grad_context, value_rows)
    row_dots = jnp.sum(probabilities * grad_probs, axis=1, keepdims=True)
    grad_scores = (probabilities * (grad_probs - row_dots)).astype(jnp.bfloat16)
    factor = 1.0 / math.sqrt(HD)
    grad_query = matmul(grad_scores, key_rows) * factor
    grad_key = matmul_first_t(grad_scores, query_rows) * factor
    grad_value = matmul_first_t(probabilities.astype(jnp.bfloat16), grad_context)
    return (grad_query, grad_key, grad_value)


def on_device(
    tokens,
    lengths,
    query_lengths,
    language_ids,
    position_table,
    segment_table,
    language_table,
    query_weight,
    key_weight,
    value_weight,
    output_weight,
    query_bias,
    value_bias,
    output_bias,
    first_gain,
    first_shift,
    up_weight,
    up_bias,
    down_weight,
    down_bias,
    second_gain,
    second_shift,
    cotangent,
):
    seq_count, seq_len, features = tokens.shape
    row_count = seq_count * seq_len
    wide_count = lax.axis_size("wide")
    narrow_count = lax.axis_size("narrow")
    attention_stacks = (
        lax.all_gather(position_table[None], ("wide", "narrow"), axis=0, tiled=True),
        lax.all_gather(query_weight[None], ("wide", "narrow"), axis=0, tiled=True),
        lax.all_gather(key_weight[None], ("wide", "narrow"), axis=0, tiled=True),
        lax.all_gather(value_weight[None], ("wide", "narrow"), axis=0, tiled=True),
        lax.all_gather(output_weight[None], ("wide", "narrow"), axis=0, tiled=True),
    )
    position_full, query_full, key_full, value_full, output_full = [
        assemble(stacked, wide_count, narrow_count) for stacked in attention_stacks
    ]
    feedforward_stacks = (
        lax.all_gather(up_weight[None], ("wide", "narrow"), axis=0, tiled=True),
        lax.all_gather(down_weight[None], ("wide", "narrow"), axis=0, tiled=True),
    )
    up_full, down_full = [
        assemble(stacked, wide_count, narrow_count) for stacked in feedforward_stacks
    ]
    places = lax.broadcasted_iota(jnp.int32, (seq_count, seq_len), 1)
    passage = (places >= query_lengths[:, None])[:, :, None]
    segment_float = segment_table.astype(jnp.float32)
    segment_rows = jnp.where(passage, segment_float[1], segment_float[0])
    language_count = language_table.shape[0]
    language_hot = (
        language_ids[:, None] == lax.broadcasted_iota(jnp.int32, (seq_count, language_count), 1)
    ).astype(jnp.bfloat16)
    language_rows = matmul(language_hot, language_table)
    start = (
        tokens.astype(jnp.float32)
        + position_full.astype(jnp.float32)[None]
        + segment_rows
        + language_rows[:, None, :]
    )
    flattened = start.reshape(row_count, features)
    first_in = flattened.astype(jnp.bfloat16)
    query_rows = (matmul(first_in, query_full) + query_bias.astype(jnp.float32)).astype(
        jnp.bfloat16
    )
    key_rows = matmul(first_in, key_full).astype(jnp.bfloat16)
    value_rows = (matmul(first_in, value_full) + value_bias.astype(jnp.float32)).astype(
        jnp.bfloat16
    )
    query_heads = split_heads(query_rows, seq_count, seq_len)
    key_heads = split_heads(key_rows, seq_count, seq_len)
    value_heads = split_heads(value_rows, seq_count, seq_len)
    head_lengths = jnp.repeat(lengths, H)
    context_blocks, log_totals = lax.map(
        attend_block, (query_heads, key_heads, value_heads, head_lengths)
    )
    context = join_heads(context_blocks, seq_count, seq_len).astype(jnp.bfloat16)
    attended = matmul(context, output_full) + output_bias.astype(jnp.float32)
    first_out, first_pull = jax.vjp(
        normalize,
        flattened + attended,
        first_gain.astype(jnp.float32),
        first_shift.astype(jnp.float32),
    )
    second_in = first_out.astype(jnp.bfloat16)
    hidden_pre = matmul(second_in, up_full) + up_bias.astype(jnp.float32)
    hidden = exact_gelu(hidden_pre).astype(jnp.bfloat16)
    branch = matmul(hidden, down_full) + down_bias.astype(jnp.float32)
    final, second_pull = jax.vjp(
        normalize,
        first_out + branch,
        second_gain.astype(jnp.float32),
        second_shift.astype(jnp.float32),
    )
    layer_out = final.astype(jnp.bfloat16).reshape(seq_count, seq_len, features)
    feedforward_again = (
        lax.all_gather(up_weight[None], ("wide", "narrow"), axis=0, tiled=True),
        lax.all_gather(down_weight[None], ("wide", "narrow"), axis=0, tiled=True),
    )
    back_up, back_down = [
        assemble(stacked, wide_count, narrow_count) for stacked in feedforward_again
    ]
    attention_again = (
        lax.all_gather(query_weight[None], ("wide", "narrow"), axis=0, tiled=True),
        lax.all_gather(key_weight[None], ("wide", "narrow"), axis=0, tiled=True),
        lax.all_gather(value_weight[None], ("wide", "narrow"), axis=0, tiled=True),
        lax.all_gather(output_weight[None], ("wide", "narrow"), axis=0, tiled=True),
    )
    back_query, back_key, back_value, back_output = [
        assemble(stacked, wide_count, narrow_count) for stacked in attention_again
    ]
    grad_second, second_gain_grad, second_shift_grad = second_pull(
        cotangent.astype(jnp.float32).reshape(row_count, features)
    )
    grad_branch = grad_second.astype(jnp.bfloat16)
    down_bias_grad = jnp.sum(grad_branch.astype(jnp.float32), axis=0)
    down_weight_grad = matmul_first_t(hidden, grad_branch)
    gelu_value, gelu_pull = jax.vjp(exact_gelu, hidden_pre)
    grad_hidden = gelu_pull(matmul_second_t(grad_branch, back_down))[0].astype(jnp.bfloat16)
    up_bias_grad = jnp.sum(grad_hidden.astype(jnp.float32), axis=0)
    up_weight_grad = matmul_first_t(second_in, grad_hidden)
    grad_first_out = grad_second + matmul_second_t(grad_hidden, back_up)
    grad_first, first_gain_grad, first_shift_grad = first_pull(grad_first_out)
    grad_attended = grad_first.astype(jnp.bfloat16)
    output_bias_grad = jnp.sum(grad_attended.astype(jnp.float32), axis=0)
    output_weight_grad = matmul_first_t(context, grad_attended)
    grad_context = matmul_second_t(grad_attended, back_output).astype(jnp.bfloat16)
    grad_query_blocks, grad_key_blocks, grad_value_blocks = lax.map(
        attend_back,
        (
            query_heads,
            key_heads,
            value_heads,
            head_lengths,
            log_totals,
            split_heads(grad_context, seq_count, seq_len),
        ),
    )
    grad_query = join_heads(grad_query_blocks, seq_count, seq_len).astype(jnp.bfloat16)
    grad_key = join_heads(grad_key_blocks, seq_count, seq_len).astype(jnp.bfloat16)
    grad_value = join_heads(grad_value_blocks, seq_count, seq_len).astype(jnp.bfloat16)
    query_bias_grad = jnp.sum(grad_query.astype(jnp.float32), axis=0)
    value_bias_grad = jnp.sum(grad_value.astype(jnp.float32), axis=0)
    query_weight_grad = matmul_first_t(first_in, grad_query)
    key_weight_grad = matmul_first_t(first_in, grad_key)
    value_weight_grad = matmul_first_t(first_in, grad_value)
    grad_start = (
        grad_first
        + matmul_second_t(grad_query, back_query)
        + matmul_second_t(grad_key, back_key)
        + matmul_second_t(grad_value, back_value)
    )
    token_grad = grad_start.astype(jnp.bfloat16).reshape(seq_count, seq_len, features)
    grad_start_pairs = grad_start.reshape(seq_count, seq_len, features)
    position_local = jnp.sum(grad_start_pairs, axis=0)
    segment_local = jnp.stack(
        [
            jnp.sum(jnp.where(passage, 0.0, grad_start_pairs), axis=(0, 1)),
            jnp.sum(jnp.where(passage, grad_start_pairs, 0.0), axis=(0, 1)),
        ]
    )
    language_local = lax.dot_general(
        language_hot.astype(jnp.float32),
        jnp.sum(grad_start_pairs, axis=1),
        (((0,), (0,)), ((), ())),
        precision=lax.Precision.HIGHEST,
    )
    attention_blocks = (
        lax.psum_scatter(
            disassemble(position_local, wide_count, narrow_count),
            ("wide", "narrow"),
            scatter_dimension=0,
            tiled=True,
        ),
        lax.psum_scatter(
            disassemble(query_weight_grad, wide_count, narrow_count),
            ("wide", "narrow"),
            scatter_dimension=0,
            tiled=True,
        ),
        lax.psum_scatter(
            disassemble(key_weight_grad, wide_count, narrow_count),
            ("wide", "narrow"),
            scatter_dimension=0,
            tiled=True,
        ),
        lax.psum_scatter(
            disassemble(value_weight_grad, wide_count, narrow_count),
            ("wide", "narrow"),
            scatter_dimension=0,
            tiled=True,
        ),
        lax.psum_scatter(
            disassemble(output_weight_grad, wide_count, narrow_count),
            ("wide", "narrow"),
            scatter_dimension=0,
            tiled=True,
        ),
    )
    attention_sums = [summed_block[0] for summed_block in attention_blocks]
    feedforward_blocks = (
        lax.psum_scatter(
            disassemble(up_weight_grad, wide_count, narrow_count),
            ("wide", "narrow"),
            scatter_dimension=0,
            tiled=True,
        ),
        lax.psum_scatter(
            disassemble(down_weight_grad, wide_count, narrow_count),
            ("wide", "narrow"),
            scatter_dimension=0,
            tiled=True,
        ),
    )
    feedforward_sums = [summed_block[0] for summed_block in feedforward_blocks]
    small_sums = lax.psum(
        (
            segment_local,
            language_local,
            query_bias_grad,
            value_bias_grad,
            output_bias_grad,
            first_gain_grad,
            first_shift_grad,
            up_bias_grad,
            down_bias_grad,
            second_gain_grad,
            second_shift_grad,
        ),
        ("wide", "narrow"),
    )
    return (
        layer_out,
        token_grad,
        attention_sums[0],
        small_sums[0],
        small_sums[1],
        attention_sums[1],
        attention_sums[2],
        attention_sums[3],
        attention_sums[4],
        small_sums[2],
        small_sums[3],
        small_sums[4],
        small_sums[5],
        small_sums[6],
        feedforward_sums[0],
        small_sums[7],
        feedforward_sums[1],
        small_sums[8],
        small_sums[9],
        small_sums[10],
    )


def solution(mesh):
    return jax.shard_map(
        on_device,
        mesh=mesh,
        in_specs=(
            P(("wide", "narrow"), None, None),
            P(("wide", "narrow")),
            P(("wide", "narrow")),
            P(("wide", "narrow")),
            P("wide", "narrow"),
            P(),
            P(),
            P("wide", "narrow"),
            P("wide", "narrow"),
            P("wide", "narrow"),
            P("wide", "narrow"),
            P(),
            P(),
            P(),
            P(),
            P(),
            P("wide", "narrow"),
            P(),
            P("wide", "narrow"),
            P(),
            P(),
            P(),
            P(("wide", "narrow"), None, None),
        ),
        out_specs=(
            P(("wide", "narrow"), None, None),
            P(("wide", "narrow"), None, None),
            P("wide", "narrow"),
            P(),
            P(),
            P("wide", "narrow"),
            P("wide", "narrow"),
            P("wide", "narrow"),
            P("wide", "narrow"),
            P(),
            P(),
            P(),
            P(),
            P(),
            P("wide", "narrow"),
            P(),
            P("wide", "narrow"),
            P(),
            P(),
            P(),
        ),
        check_vma=False,
    )
```

profile of v0, /device:TPU:0, one launch (start us, length us, event | category | flops | bytes accessed | tf_op | source)
XLA Modules:
  0.0 2180.7 jit_solution(14981579719575982084)
XLA Ops:
  12.8 79.9 %all-gather = bf16[2048,192]{1,0:T(8,128)(2,1)S(1)} all-gather(bf16[64,192]{1,0:T(8,128)(2,1)} %param.31), channel_id=2, replica_groups=mesh['wide'=8,'narrow'=4] {'wide','narrow'}, dimensions={0}, use_global_device_ids=true | all-gather | bytes 811008 | tf_op jit(solution)/shard_map/all_gather | solution.py:137
  98.9 6.5 fusion.60
  123.1 7.7 copy.107
  148.6 7.7 copy.109
  156.3 27.0 %all-gather.16.cloned.1.call-done = bf16[3072,192]{1,0:T(8,128)(2,1)} async-done(((bf16[96,192]{1,0:T(8,128)(2,1)}), bf16[3072,192]{1,0:T(8,128)(2,1)}) %all-gather.16.cloned.1.call-update) | async-done | bytes 1179664 | tf_op jit(solution)/shard_map/all_gather | solution.py:139
  201.2 7.7 copy.108
  209.3 255.0 %while.26 = (s32[]{:T(128)}, bf16[48,512,64]{1,2,0:T(8,128)(2,1)S(1)}, f32[48,512]{1,0:T(8,128)}, s32[48]{0:T(128)S(1)}, bf16[48,512,64]{2,1,0:T(8,128)(2,1)}, /...) while((s32[]{:T(128)}, bf16[48,512,64]{1,2,0:T(8,128)(2,1)S(1)}, ...), condition=%wide.region_3.4_spmd, body=%wide.region_0.3_spmd.sunk | while | flops 69206016 | bytes 3693681 | solution.py:181
  473.0 7.5 fusion.69
  493.4 8.2 reshape.353
  509.4 68.8 %multiply_convert_fusion.1 = (bf16[2048,3072]{1,0:T(8,128)(2,1)}, f32[2048,3072]{1,0:T(8,128)}, f32[2048,3072]{1,0:T(8,128)}) fusion(f32[3072]{0:T(1024)S(1)} %convert_element_type.206, bf16[768,3072]{1,0:T(8,128)(2,1)S(1)} %bitcast.362, f32[2048,768]{1,0:T(8,128)S(1)} %bitcast.331, f32[768]{0:T(1024)S(1)} %convert_element_type.204, ...), kind=kOutput, calls=%fused_computation.60 | convolution fusion | flops 10086776832 | bytes 73959424 | tf_op jit(solution)/shard_map/dot_general | solution.py:20
  578.2 15.1 fusion.70
  606.4 29.2 %convert_reduce_fusion = (f32[3072]{0:T(1024)}, bf16[2048,3072]{1,0:T(8,128)(2,1)}) fusion(f32[2048,3072]{1,0:T(8,128)} %get-tuple-element.196, bf16[2048,768]{1,0:T(8,128)(2,1)S(1)} %get-tuple-element.188, bf16[3072,768]{0,1:T(8,128)(2,1)} %bitcast.364, f32[2048,3072]{1,0:T(8,128)} %get-tuple-element.209, f32[3072]{0:T(1024)S(1)} %convert_element_type.206), kind=kOutput, calls=%fused_computation.58 | convolution fusion | flops 9770628096 | bytes 70803456 | tf_op jit(solution)/shard_map/dot_general | solution.py:30
  635.7 19.3 multiply_reduce_fusion.1
  675.5 7.7 copy.112
  687.6 467.8 %while.27 = (s32[]{:T(128)}, bf16[48,512,64]{1,2,0:T(8,128)(2,1)S(1)}, bf16[48,512,64]{1,2,0:T(8,128)(2,1)}, bf16[48,512,64]{1,2,0:T(8,128)(2,1)}, s32[48]{0:T(1...) while((s32[]{:T(128)}, ...), condition=%wide.region_14.15_spmd, body=%wide.region_12.14_spmd.sunk | while | flops 170196992 | bytes 9191553 | solution.py:235
  1177.7 9.6 select_reduce_fusion.1
  1191.5 8.0 fusion.76
  1220.7 8.0 fusion.73
  1228.8 7.9 fusion.74
  1236.8 8.0 fusion.75
  1244.8 16.4 fusion.77
  1273.2 18.6 fusion.61
  1291.8 12.7 reshape.367
  1304.5 9.0 copy.101
  1324.9 40.7 %all-reduce = (f32[2,768]{1,0:T(2,128)}, f32[768]{0:T(1024)}, f32[768]{0:T(1024)}, f32[768]{0:T(1024)}, f32[768]{0:T(1024)}, /*index=5*/f32[768]{0:T(1024)}, f32...) all-reduce(f32[2,768]{1,0:T(2,128)S(1)} %pad_maximum_fusion, ...), channel_id=1, replica_groups=mesh['wide'=8,'narrow'=4] {'wide','narrow'}, use_global_device_ids=true, to_apply=%region_19.20 | all-reduce | flops 10752 | bytes 86016 | tf_op jit(solution)/shard_map/psum | solution.py:323
  1365.6 61.2 %reduce-scatter.16.cloned.1.call-done = f32[1,96,192]{2,1,0:T(8,128)} async-done(((f32[32,96,192]{2,1,0:T(8,128)}), f32[1,96,192]{2,1,0:T(8,128)}) %reduce-scatter.16.cloned.1.call-update) | async-done | bytes 73744 | tf_op jit(solution)/shard_map/reduce_scatter | solution.py:300
  1426.8 142.0 %reduce-scatter.8.cloned.1.call-done = f32[1,64,192]{2,1,0:T(8,128)} async-done(((f32[32,64,192]{2,1,0:T(8,128)}), f32[1,64,192]{2,1,0:T(8,128)}) %reduce-scatter.8.cloned.1.call-update) | async-done | bytes 49168 | tf_op jit(solution)/shard_map/reduce_scatter | solution.py:276
  1568.8 105.7 %reduce-scatter.10.cloned.1.call-done = f32[1,96,192]{2,1,0:T(8,128)} async-done(((f32[32,96,192]{2,1,0:T(8,128)}), f32[1,96,192]{2,1,0:T(8,128)}) %reduce-scatter.10.cloned.1.call-update) | async-done | bytes 73744 | tf_op jit(solution)/shard_map/reduce_scatter | solution.py:282
  1674.4 107.2 %reduce-scatter.12.cloned.1.call-done = f32[1,96,192]{2,1,0:T(8,128)} async-done(((f32[32,96,192]{2,1,0:T(8,128)}), f32[1,96,192]{2,1,0:T(8,128)}) %reduce-scatter.12.cloned.1.call-update) | async-done | bytes 73744 | tf_op jit(solution)/shard_map/reduce_scatter | solution.py:288
  1781.7 107.1 %reduce-scatter.14.cloned.1.call-done = f32[1,96,192]{2,1,0:T(8,128)} async-done(((f32[32,96,192]{2,1,0:T(8,128)}), f32[1,96,192]{2,1,0:T(8,128)}) %reduce-scatter.14.cloned.1.call-update) | async-done | bytes 73744 | tf_op jit(solution)/shard_map/reduce_scatter | solution.py:294
  1888.7 141.7 %reduce-scatter.20.cloned.1.call-done = f32[1,384,192]{1,2,0:T(8,128)} async-done(((f32[32,384,192]{1,2,0:T(8,128)}), f32[1,384,192]{1,2,0:T(8,128)}) %reduce-scatter.20.cloned.1.call-update) | async-done | bytes 294928 | tf_op jit(solution)/shard_map/reduce_scatter | solution.py:315
  2030.4 141.5 %reduce-scatter.18.cloned.1.call-done = f32[1,96,768]{2,1,0:T(8,128)} async-done(((f32[32,96,768]{2,1,0:T(8,128)}), f32[1,96,768]{2,1,0:T(8,128)}) %reduce-scatter.18.cloned.1.call-update) | async-done | bytes 294928 | tf_op jit(solution)/shard_map/reduce_scatter | solution.py:309
  (1001 shorter events, 925.2 us)
Async XLA Ops:
  7.2 91.5 %copy-start = (bf16[100,768]{1,0:T(8,128)(2,1)S(1)}, bf16[100,768]{1,0:T(8,128)(2,1)}, u32[]{:S(2)}) copy-start(bf16[100,768]{1,0:T(8,128)(2,1)} %param.33) | copy-start | bytes 460804
  7.2 88.8 %copy-start.36 = (bf16[768]{0:T(1024)(128)(2,1)S(1)}, bf16[768]{0:T(1024)(128)(2,1)}, u32[]{:S(2)}) copy-start(bf16[768]{0:T(1024)(128)(2,1)} %param.38) | copy-start | bytes 4612
  7.2 88.8 %copy-start.37 = (bf16[768]{0:T(1024)(128)(2,1)S(1)}, bf16[768]{0:T(1024)(128)(2,1)}, u32[]{:S(2)}) copy-start(bf16[768]{0:T(1024)(128)(2,1)} %param.39) | copy-start | bytes 4612
  7.2 88.8 %copy-start.46 = (s32[4]{0:T(128)S(1)}, s32[4]{0:T(128)}, u32[]{:S(2)}) copy-start(s32[4]{0:T(128)} %param.28) | copy-start | bytes 52
  7.2 89.0 %copy-start.38 = (bf16[768]{0:T(1024)(128)(2,1)S(1)}, bf16[768]{0:T(1024)(128)(2,1)}, u32[]{:S(2)}) copy-start(bf16[768]{0:T(1024)(128)(2,1)} %param.40) | copy-start | bytes 4612
  7.2 89.0 %copy-start.39 = (bf16[768]{0:T(1024)(128)(2,1)S(1)}, bf16[768]{0:T(1024)(128)(2,1)}, u32[]{:S(2)}) copy-start(bf16[768]{0:T(1024)(128)(2,1)} %param.41) | copy-start | bytes 4612
  7.3 89.0 %copy-start.40 = (bf16[768]{0:T(1024)(128)(2,1)S(1)}, bf16[768]{0:T(1024)(128)(2,1)}, u32[]{:S(2)}) copy-start(bf16[768]{0:T(1024)(128)(2,1)} %param.42) | copy-start | bytes 4612
  7.3 89.0 %copy-start.30 = (bf16[3072]{0:T(1024)(128)(2,1)S(1)}, bf16[3072]{0:T(1024)(128)(2,1)}, u32[]{:S(2)}) copy-start(bf16[3072]{0:T(1024)(128)(2,1)} %param.44) | copy-start | bytes 18436
  7.3 89.0 %copy-start.41 = (bf16[768]{0:T(1024)(128)(2,1)S(1)}, bf16[768]{0:T(1024)(128)(2,1)}, u32[]{:S(2)}) copy-start(bf16[768]{0:T(1024)(128)(2,1)} %param.46) | copy-start | bytes 4612
  7.3 89.6 %copy-start.42 = (bf16[768]{0:T(1024)(128)(2,1)S(1)}, bf16[768]{0:T(1024)(128)(2,1)}, u32[]{:S(2)}) copy-start(bf16[768]{0:T(1024)(128)(2,1)} %param.47) | copy-start | bytes 4612
  7.3 90.2 %copy-start.43 = (bf16[768]{0:T(1024)(128)(2,1)S(1)}, bf16[768]{0:T(1024)(128)(2,1)}, u32[]{:S(2)}) copy-start(bf16[768]{0:T(1024)(128)(2,1)} %param.48) | copy-start | bytes 4612
  7.3 91.4 %copy-start.44 = (s32[4]{0:T(128)S(1)}, s32[4]{0:T(128)}, u32[]{:S(2)}) copy-start(s32[4]{0:T(128)} %param.30) | copy-start | bytes 52
  7.3 98.0 %all-gather.14.cloned.1.call-start = ((), (), s32[]{:S(2)}) async-start(), calls=%async_computation.15 | async-start | bytes 1622016 | tf_op jit(solution)/shard_map/all_gather | solution.py:138
  8.1 122.7 %all-gather.18.cloned.1.call-start = ((), (), s32[]{:S(2)}) async-start(), calls=%async_computation.17 | async-start | bytes 1622016 | tf_op jit(solution)/shard_map/all_gather | solution.py:140
  8.8 174.5 %all-gather.16.cloned.1.call-start = ((), (), s32[]{:S(2)}) async-start(), calls=%async_computation.16 | async-start | bytes 1622016 | tf_op jit(solution)/shard_map/all_gather | solution.py:139
  9.5 459.9 %all-gather.20.cloned.1.call-start = ((), (), s32[]{:S(2)}) async-start(), calls=%async_computation.18 | async-start | bytes 1622016 | tf_op jit(solution)/shard_map/all_gather | solution.py:141
  10.1 474.1 %all-gather.22.cloned.1.call-start = ((), (), s32[]{:S(2)}) async-start(), calls=%async_computation.19 | async-start | bytes 4866048 | tf_op jit(solution)/shard_map/all_gather | solution.py:147
  10.7 482.7 %all-gather.24.cloned.1.call-start = ((), (), s32[]{:S(2)}) async-start(), calls=%async_computation.20 | async-start | bytes 4866048 | tf_op jit(solution)/shard_map/all_gather | solution.py:148
  11.3 1354.3 %all-reduce.3.cloned.1.call-start = ((), (), s32[]{:S(2)}) async-start(), calls=%async_computation.8 | async-start | bytes 638976 | tf_op jit(solution)/shard_map/psum | solution.py:323
  96.3 481.9 %copy-start.33 = (f32[768]{0:T(1024)}, f32[768]{0:T(1024)S(1)}, u32[]{:S(2)}) copy-start(f32[768]{0:T(1024)S(1)} %convert_element_type.204) | copy-start | bytes 9220
  509.4 68.8 %copy-start.35 = (f32[768]{0:T(1024)S(1)}, f32[768]{0:T(1024)}, u32[]{:S(2)}) copy-start(f32[768]{0:T(1024)} %convert_element_type.208) | copy-start | bytes 9220
  606.4 29.2 %copy-start.12 = (bf16[2048,768]{1,0:T(8,128)(2,1)}, bf16[2048,768]{1,0:T(8,128)(2,1)S(1)}, u32[]{:S(2)}) copy-start(bf16[2048,768]{1,0:T(8,128)(2,1)S(1)} %get-tuple-element.188) | copy-start | bytes 9437188
  635.7 19.3 copy-start.22
  1166.1 11.6 slice-start
  1191.5 235.3 %reduce-scatter.16.cloned.1.call-start = ((), (), s32[]{:S(2)}) async-start(), calls=%async_computation.12 | async-start | bytes 3244032 | tf_op jit(solution)/shard_map/reduce_scatter | solution.py:300
  1199.5 369.2 %reduce-scatter.8.cloned.1.call-start = ((), (), s32[]{:S(2)}) async-start(), calls=%async_computation.7 | async-start | bytes 2162688 | tf_op jit(solution)/shard_map/reduce_scatter | solution.py:276
  1211.2 463.2 %reduce-scatter.10.cloned.1.call-start = ((), (), s32[]{:S(2)}) async-start(), calls=%async_computation.9 | async-start | bytes 3244032 | tf_op jit(solution)/shard_map/reduce_scatter | solution.py:282
  1228.8 552.9 %reduce-scatter.12.cloned.1.call-start = ((), (), s32[]{:S(2)}) async-start(), calls=%async_computation.10 | async-start | bytes 3244032 | tf_op jit(solution)/shard_map/reduce_scatter | solution.py:288
  1236.8 652.0 %reduce-scatter.14.cloned.1.call-start = ((), (), s32[]{:S(2)}) async-start(), calls=%async_computation.11 | async-start | bytes 3244032 | tf_op jit(solution)/shard_map/reduce_scatter | solution.py:294
  1244.8 785.6 %reduce-scatter.20.cloned.1.call-start = ((), (), s32[]{:S(2)}) async-start(), calls=%async_computation.14 | async-start | bytes 9732096 | tf_op jit(solution)/shard_map/reduce_scatter | solution.py:315
  1272.5 899.4 %reduce-scatter.18.cloned.1.call-start = ((), (), s32[]{:S(2)}) async-start(), calls=%async_computation.13 | async-start | bytes 9732096 | tf_op jit(solution)/shard_map/reduce_scatter | solution.py:309
  1313.6 860.0 %copy-start.1 = (bf16[100,768]{1,0:T(8,128)(2,1)S(1)}, bf16[100,768]{1,0:T(8,128)(2,1)}, u32[]{:S(2)}) copy-start(bf16[100,768]{1,0:T(8,128)(2,1)} %param.33) | copy-start | bytes 460804
  (35 other events, 192.6 us)
Sparse Core Ops, SparseCore 0:
  11.0 58.6 all-gather.13
  72.6 53.8 all-gather.17
  129.4 53.8 all-gather.15
  186.1 53.9 all-gather.19
  242.7 62.4 all-gather.21
  307.9 61.8 all-gather.23
  1191.6 125.9 all-reduce.2
  1323.6 103.1 reduce-scatter.15
  1429.6 139.1 reduce-scatter.7
  1574.6 99.7 reduce-scatter.9
  1680.4 101.1 reduce-scatter.11
  1787.5 101.1 reduce-scatter.13
  1895.2 135.1 reduce-scatter.19
  2036.7 135.1 reduce-scatter.17
where the time goes:
time: 2200 us; the launch traced here: 2180 us
  waiting for transfers between devices  837 us (38%)
  matrix products  730 us (33%)
  local copies, waits for them, and re-layouts  344 us (16%)
  other arithmetic  131 us (6%)
  blocking collectives  121 us (6%)
    dot_general x150, matrix products, matmul_second_t(): lax.dot_general(left_side, right_side, (((1,), (1,)), ((), ())), preferre...  262 us
    dot_general x102, matrix products, matmul_first_t(): lax.dot_general(left_side, right_side, (((0,), (0,)), ((), ())), preferre...  243 us
    dot_general x103, matrix products, matmul(): return jnp.dot(left_side, right_side, preferred_element_type=jnp.float32)  224 us
    reduce_scatter x1, waiting for transfers between devices, on_device(): lax.psum_scatter(disassemble(position_local, wide_count, narrow_count), (...  142 us
    reduce_scatter x1, waiting for transfers between devices, on_device(): lax.psum_scatter(disassemble(down_weight_grad, wide_count, narrow_count),...  142 us
    reduce_scatter x1, waiting for transfers between devices, on_device(): lax.psum_scatter(disassemble(up_weight_grad, wide_count, narrow_count), (...  141 us
    reduce_scatter x1, waiting for transfers between devices, on_device(): lax.psum_scatter(disassemble(key_weight_grad, wide_count, narrow_count),...  107 us
    reduce_scatter x1, waiting for transfers between devices, on_device(): lax.psum_scatter(disassemble(value_weight_grad, wide_count, narrow_count)...  107 us
  transfers between devices with their start and end apart: 14, of which 8 were waited for; matrix products, arithmetic and copies ran while one was open for 23% of the time, Pallas kernels for 0%

commit v1 on v0

--- a/solution.py
+++ b/solution.py
@@ -133,8 +133,27 @@
     row_count = seq_count * seq_len
     wide_count = lax.axis_size("wide")
     narrow_count = lax.axis_size("narrow")
+
+    def point_modes_on_mesh(x_local, which_dim):
+        link_axis = ("wide", "narrow")
+        work_now = lax.axis_size(link_axis)
+        tmp, view_out = (work_now, lax.axis_index(link_axis))
+        b_now, u_next = (x_local, 1)
+        while u_next < tmp:
+            stack_in = []
+            nth = 0
+            while nth < tmp:
+                stack_in.append((nth, nth ^ u_next))
+                nth = nth + 1
+            finding = lax.ppermute(b_now, link_axis, stack_in)
+            y = jnp.concatenate([b_now, finding], which_dim)
+            answer = jnp.concatenate([finding, b_now], axis=which_dim)
+            b_now = jnp.where(view_out & u_next == 0, y, answer)
+            u_next = 2 * u_next
+        return b_now
+
     attention_stacks = (
-        lax.all_gather(position_table[None], ("wide", "narrow"), axis=0, tiled=True),
+        point_modes_on_mesh(position_table[None], 0),
         lax.all_gather(query_weight[None], ("wide", "narrow"), axis=0, tiled=True),
         lax.all_gather(key_weight[None], ("wide", "narrow"), axis=0, tiled=True),
         lax.all_gather(value_weight[None], ("wide", "narrow"), axis=0, tiled=True),

time: 2200 us -> 2200 us (level)
  blocking collectives: 121 us -> 40.6 us
  waiting for transfers between devices: 837 us -> 898 us
    all_gather x1 -> x0, blocking collectives: 79.9 us -> none  [on_device(): lax.all_gather(position_table[None], ('wide', 'narrow'), axis=0, tiled=True)]
    all_gather x1, waiting for transfers between devices: 0.01 us -> 31.4 us  [on_device(): lax.all_gather(value_weight[None], ('wide', 'narrow'), axis=0, tiled=True)]
  transfers between devices with their start and end apart: 14 -> 19, of which waited for: 8 -> 15; matrix products, arithmetic and copies ran while one was open for 23% -> 23% of each run, Pallas kernels for 0% -> 0%
where the time goes in v1:
time: 2200 us; the launch traced here: 2180 us
  waiting for transfers between devices  898 us (41%)
  matrix products  730 us (33%)
  local copies, waits for them, and re-layouts  344 us (16%)
  other arithmetic  139 us (6%)
  blocking collectives  40.6 us (2%)
    dot_general x150, matrix products, matmul_second_t(): lax.dot_general(left_side, right_side, (((1,), (1,)), ((), ())), preferre...  262 us
    dot_general x102, matrix products, matmul_first_t(): lax.dot_general(left_side, right_side, (((0,), (0,)), ((), ())), preferre...  243 us
    dot_general x103, matrix products, matmul(): return jnp.dot(left_side, right_side, preferred_element_type=jnp.float32)  224 us
    reduce_scatter x1, waiting for transfers between devices, on_device(): lax.psum_scatter(disassemble(position_local, wide_count, narrow_count), (...  142 us
    reduce_scatter x1, waiting for transfers between devices, on_device(): lax.psum_scatter(disassemble(down_weight_grad, wide_count, narrow_count),...  142 us
    reduce_scatter x1, waiting for transfers between devices, on_device(): lax.psum_scatter(disassemble(up_weight_grad, wide_count, narrow_count), (...  141 us
    reduce_scatter x1, waiting for transfers between devices, on_device(): lax.psum_scatter(disassemble(key_weight_grad, wide_count, narrow_count),...  107 us
    reduce_scatter x1, waiting for transfers between devices, on_device(): lax.psum_scatter(disassemble(value_weight_grad, wide_count, narrow_count)...  107 us
  transfers between devices with their start and end apart: 19, of which 15 were waited for; matrix products, arithmetic and copies ran while one was open for 23% of the time, Pallas kernels for 0%

profile of v1, /device:TPU:0, one launch (start us, length us, event | category | flops | bytes accessed | tf_op | source)
XLA Modules:
  0.0 2179.9 jit_solution(790534939612973937)
XLA Ops:
  56.5 12.3 all-gather.13.cloned.1.call-done
  86.5 7.7 copy.107
  94.2 31.4 %all-gather.17.cloned.1.call-done = bf16[3072,192]{1,0:T(8,128)(2,1)} async-done(((bf16[96,192]{1,0:T(8,128)(2,1)}), bf16[3072,192]{1,0:T(8,128)(2,1)}) %all-gather.17.cloned.1.call-update) | async-done | bytes 1179664 | tf_op jit(solution)/shard_map/all_gather | solution.py:159
  143.4 7.7 copy.109
  151.1 31.3 %all-gather.15.cloned.1.call-done = bf16[3072,192]{1,0:T(8,128)(2,1)} async-done(((bf16[96,192]{1,0:T(8,128)(2,1)}), bf16[3072,192]{1,0:T(8,128)(2,1)}) %all-gather.15.cloned.1.call-update) | async-done | bytes 1179664 | tf_op jit(solution)/shard_map/all_gather | solution.py:158
  200.3 7.7 copy.108
  208.4 255.0 %while.26 = (s32[]{:T(128)}, bf16[48,512,64]{1,2,0:T(8,128)(2,1)S(1)}, f32[48,512]{1,0:T(8,128)}, s32[48]{0:T(128)S(1)}, bf16[48,512,64]{2,1,0:T(8,128)(2,1)}, /...) while((s32[]{:T(128)}, bf16[48,512,64]{1,2,0:T(8,128)(2,1)S(1)}, ...), condition=%wide.region_3.4_spmd, body=%wide.region_0.3_spmd.sunk | while | flops 69206016 | bytes 3693681 | solution.py:200
  472.1 7.5 fusion.69
  492.4 8.2 reshape.357
  508.5 68.8 %multiply_convert_fusion.1 = (bf16[2048,3072]{1,0:T(8,128)(2,1)}, f32[2048,3072]{1,0:T(8,128)}, f32[2048,3072]{1,0:T(8,128)}) fusion(f32[3072]{0:T(1024)S(1)} %convert_element_type.206, bf16[768,3072]{1,0:T(8,128)(2,1)S(1)} %bitcast.363, f32[2048,768]{1,0:T(8,128)S(1)} %bitcast.332, f32[768]{0:T(1024)S(1)} %convert_element_type.204, ...), kind=kOutput, calls=%fused_computation.60 | convolution fusion | flops 10086776832 | bytes 73959424 | tf_op jit(solution)/shard_map/dot_general | solution.py:20
  577.3 15.1 fusion.70
  605.5 29.2 %convert_reduce_fusion = (f32[3072]{0:T(1024)}, bf16[2048,3072]{1,0:T(8,128)(2,1)}) fusion(f32[2048,3072]{1,0:T(8,128)} %get-tuple-element.196, bf16[2048,768]{1,0:T(8,128)(2,1)S(1)} %get-tuple-element.188, bf16[3072,768]{0,1:T(8,128)(2,1)} %bitcast.365, f32[2048,3072]{1,0:T(8,128)} %get-tuple-element.209, f32[3072]{0:T(1024)S(1)} %convert_element_type.206), kind=kOutput, calls=%fused_computation.58 | convolution fusion | flops 9770628096 | bytes 70803456 | tf_op jit(solution)/shard_map/dot_general | solution.py:30
  634.8 19.2 multiply_reduce_fusion.1
  674.6 7.7 copy.112
  686.7 467.7 %while.27 = (s32[]{:T(128)}, bf16[48,512,64]{1,2,0:T(8,128)(2,1)S(1)}, bf16[48,512,64]{1,2,0:T(8,128)(2,1)}, bf16[48,512,64]{1,2,0:T(8,128)(2,1)}, s32[48]{0:T(1...) while((s32[]{:T(128)}, ...), condition=%wide.region_14.15_spmd, body=%wide.region_12.14_spmd.sunk | while | flops 170196992 | bytes 9191553 | solution.py:254
  1176.7 9.6 select_reduce_fusion.1
  1190.5 8.0 fusion.76
  1219.7 8.0 fusion.73
  1227.8 7.9 fusion.74
  1235.8 8.0 fusion.75
  1243.9 16.4 fusion.77
  1272.2 18.5 fusion.61
  1290.7 12.7 reshape.371
  1303.4 9.1 copy.101
  1323.9 40.6 %all-reduce = (f32[2,768]{1,0:T(2,128)}, f32[768]{0:T(1024)}, f32[768]{0:T(1024)}, f32[768]{0:T(1024)}, f32[768]{0:T(1024)}, /*index=5*/f32[768]{0:T(1024)}, f32...) all-reduce(f32[2,768]{1,0:T(2,128)S(1)} %pad_maximum_fusion, ...), channel_id=1, replica_groups=mesh['wide'=8,'narrow'=4] {'wide','narrow'}, use_global_device_ids=true, to_apply=%region_19.20 | all-reduce | flops 10752 | bytes 86016 | tf_op jit(solution)/shard_map/psum | solution.py:342
  1364.5 61.3 %reduce-scatter.16.cloned.1.call-done = f32[1,96,192]{2,1,0:T(8,128)} async-done(((f32[32,96,192]{2,1,0:T(8,128)}), f32[1,96,192]{2,1,0:T(8,128)}) %reduce-scatter.16.cloned.1.call-update) | async-done | bytes 73744 | tf_op jit(solution)/shard_map/reduce_scatter | solution.py:319
  1425.8 142.2 %reduce-scatter.8.cloned.1.call-done = f32[1,64,192]{2,1,0:T(8,128)} async-done(((f32[32,64,192]{2,1,0:T(8,128)}), f32[1,64,192]{2,1,0:T(8,128)}) %reduce-scatter.8.cloned.1.call-update) | async-done | bytes 49168 | tf_op jit(solution)/shard_map/reduce_scatter | solution.py:295
  1568.0 105.7 %reduce-scatter.10.cloned.1.call-done = f32[1,96,192]{2,1,0:T(8,128)} async-done(((f32[32,96,192]{2,1,0:T(8,128)}), f32[1,96,192]{2,1,0:T(8,128)}) %reduce-scatter.10.cloned.1.call-update) | async-done | bytes 73744 | tf_op jit(solution)/shard_map/reduce_scatter | solution.py:301
  1673.7 107.2 %reduce-scatter.12.cloned.1.call-done = f32[1,96,192]{2,1,0:T(8,128)} async-done(((f32[32,96,192]{2,1,0:T(8,128)}), f32[1,96,192]{2,1,0:T(8,128)}) %reduce-scatter.12.cloned.1.call-update) | async-done | bytes 73744 | tf_op jit(solution)/shard_map/reduce_scatter | solution.py:307
  1780.9 107.1 %reduce-scatter.14.cloned.1.call-done = f32[1,96,192]{2,1,0:T(8,128)} async-done(((f32[32,96,192]{2,1,0:T(8,128)}), f32[1,96,192]{2,1,0:T(8,128)}) %reduce-scatter.14.cloned.1.call-update) | async-done | bytes 73744 | tf_op jit(solution)/shard_map/reduce_scatter | solution.py:313
  1888.0 141.7 %reduce-scatter.20.cloned.1.call-done = f32[1,384,192]{1,2,0:T(8,128)} async-done(((f32[32,384,192]{1,2,0:T(8,128)}), f32[1,384,192]{1,2,0:T(8,128)}) %reduce-scatter.20.cloned.1.call-update) | async-done | bytes 294928 | tf_op jit(solution)/shard_map/reduce_scatter | solution.py:334
  2029.7 141.5 %reduce-scatter.18.cloned.1.call-done = f32[1,96,768]{2,1,0:T(8,128)} async-done(((f32[32,96,768]{2,1,0:T(8,128)}), f32[1,96,768]{2,1,0:T(8,128)}) %reduce-scatter.18.cloned.1.call-update) | async-done | bytes 294928 | tf_op jit(solution)/shard_map/reduce_scatter | solution.py:328
  (993 shorter events, 962.7 us)
Async XLA Ops:
  7.2 37.8 %copy-start = (bf16[100,768]{1,0:T(8,128)(2,1)S(1)}, bf16[100,768]{1,0:T(8,128)(2,1)}, u32[]{:S(2)}) copy-start(bf16[100,768]{1,0:T(8,128)(2,1)} %param.33) | copy-start | bytes 460804
  7.2 61.6 %all-gather.13.cloned.1.call-start = ((), (), s32[]{:S(2)}) async-start(), calls=%async_computation.15 | async-start | bytes 1622016 | tf_op jit(solution)/shard_map/all_gather | solution.py:157
  7.9 117.7 %all-gather.17.cloned.1.call-start = ((), (), s32[]{:S(2)}) async-start(), calls=%async_computation.17 | async-start | bytes 1622016 | tf_op jit(solution)/shard_map/all_gather | solution.py:159
  8.7 173.8 %all-gather.15.cloned.1.call-start = ((), (), s32[]{:S(2)}) async-start(), calls=%async_computation.16 | async-start | bytes 1622016 | tf_op jit(solution)/shard_map/all_gather | solution.py:158
  9.4 459.1 %all-gather.19.cloned.1.call-start = ((), (), s32[]{:S(2)}) async-start(), calls=%async_computation.18 | async-start | bytes 1622016 | tf_op jit(solution)/shard_map/all_gather | solution.py:160
  10.0 473.2 %all-gather.21.cloned.1.call-start = ((), (), s32[]{:S(2)}) async-start(), calls=%async_computation.19 | async-start | bytes 4866048 | tf_op jit(solution)/shard_map/all_gather | solution.py:166
  10.6 481.8 %all-gather.23.cloned.1.call-start = ((), (), s32[]{:S(2)}) async-start(), calls=%async_computation.20 | async-start | bytes 4866048 | tf_op jit(solution)/shard_map/all_gather | solution.py:167
  10.6 5.2 collective-permute-start
  16.7 5.3 collective-permute-start.1
  22.1 1.4 collective-permute-start.2
  23.6 8.5 collective-permute-start.3
  25.5 1339.0 %all-reduce.3.cloned.1.call-start = ((), (), s32[]{:S(2)}) async-start(), calls=%async_computation.8 | async-start | bytes 638976 | tf_op jit(solution)/shard_map/psum | solution.py:342
  32.3 14.0 collective-permute-start.4
  39.8 537.4 %copy-start.32 = (f32[768]{0:T(1024)}, f32[768]{0:T(1024)S(1)}, u32[]{:S(2)}) copy-start(f32[768]{0:T(1024)S(1)} %convert_element_type.204) | copy-start | bytes 9220
  508.5 68.8 %copy-start.34 = (f32[768]{0:T(1024)S(1)}, f32[768]{0:T(1024)}, u32[]{:S(2)}) copy-start(f32[768]{0:T(1024)} %convert_element_type.208) | copy-start | bytes 9220
  605.5 29.2 %copy-start.12 = (bf16[2048,768]{1,0:T(8,128)(2,1)}, bf16[2048,768]{1,0:T(8,128)(2,1)S(1)}, u32[]{:S(2)}) copy-start(bf16[2048,768]{1,0:T(8,128)(2,1)S(1)} %get-tuple-element.188) | copy-start | bytes 9437188
  634.8 19.2 copy-start.22
  1165.0 11.6 slice-start
  1190.5 235.4 %reduce-scatter.16.cloned.1.call-start = ((), (), s32[]{:S(2)}) async-start(), calls=%async_computation.12 | async-start | bytes 3244032 | tf_op jit(solution)/shard_map/reduce_scatter | solution.py:319
  1198.5 369.4 %reduce-scatter.8.cloned.1.call-start = ((), (), s32[]{:S(2)}) async-start(), calls=%async_computation.7 | async-start | bytes 2162688 | tf_op jit(solution)/shard_map/reduce_scatter | solution.py:295
  1210.3 463.4 %reduce-scatter.10.cloned.1.call-start = ((), (), s32[]{:S(2)}) async-start(), calls=%async_computation.9 | async-start | bytes 3244032 | tf_op jit(solution)/shard_map/reduce_scatter | solution.py:301
  1227.8 553.1 %reduce-scatter.12.cloned.1.call-start = ((), (), s32[]{:S(2)}) async-start(), calls=%async_computation.10 | async-start | bytes 3244032 | tf_op jit(solution)/shard_map/reduce_scatter | solution.py:307
  1235.8 652.2 %reduce-scatter.14.cloned.1.call-start = ((), (), s32[]{:S(2)}) async-start(), calls=%async_computation.11 | async-start | bytes 3244032 | tf_op jit(solution)/shard_map/reduce_scatter | solution.py:313
  1243.8 785.9 %reduce-scatter.20.cloned.1.call-start = ((), (), s32[]{:S(2)}) async-start(), calls=%async_computation.14 | async-start | bytes 9732096 | tf_op jit(solution)/shard_map/reduce_scatter | solution.py:334
  1271.5 899.7 %reduce-scatter.18.cloned.1.call-start = ((), (), s32[]{:S(2)}) async-start(), calls=%async_computation.13 | async-start | bytes 9732096 | tf_op jit(solution)/shard_map/reduce_scatter | solution.py:328
  1312.5 11.3 copy-start.24
  1312.5 11.3 copy-start.25
  1312.5 11.3 copy-start.26
  1312.5 11.3 copy-start.28
  1312.5 11.3 copy-start.30
  1312.6 11.3 copy-start.31
  1312.6 860.3 %copy-start.1 = (bf16[100,768]{1,0:T(8,128)(2,1)S(1)}, bf16[100,768]{1,0:T(8,128)(2,1)}, u32[]{:S(2)}) copy-start(bf16[100,768]{1,0:T(8,128)(2,1)} %param.33) | copy-start | bytes 460804
  (29 other events, 124.9 us)
Sparse Core Ops, SparseCore 0:
  10.9 57.8 all-gather.12
  71.7 53.8 all-gather.16
  128.5 53.8 all-gather.14
  185.2 53.9 all-gather.18
  241.8 62.4 all-gather.20
  307.0 62.0 all-gather.22
  1190.6 126.0 all-reduce.2
  1322.7 103.1 reduce-scatter.15
  1428.7 139.2 reduce-scatter.7
  1573.8 99.8 reduce-scatter.9
  1679.7 101.1 reduce-scatter.11
  1786.8 101.1 reduce-scatter.13
  1894.5 135.1 reduce-scatter.19
  2036.0 135.1 reduce-scatter.17
